TPU v7x, 128 devices: a whole 4x4x4 slice. The times are simulated.
128 devices in a mesh: lat: 8 (over z, core), lon: 16 (over y, x).
Axes of the slice: x: 4, y: 4, z: 4, core: 2. Of those that a mesh axis runs over, the one named last changes fastest.
Arguments:
- control: float32 [254, 64, 1536], P(None, 'lat', 'lon'), may hold values from -6 to 6
- vert_band: float32 [2, 9, 127], replicated, may hold values from -2.5 to 2.5
- lat_length: float32 [254, 8], replicated, may hold values from 3 to 32
- lon_length: float32 [254], replicated, may hold values from 3 to 192
- band_index: int32 [64], replicated, may hold values from 0 to 7
- owner_device: int32 [254, 1], replicated, may hold values from 0 to 127; in each aligned block of 254 rows (0 to 253, 254 to 507, ...) at most 4 rows name the same one
Outputs:
- winds: float32 [254, 64, 1536], P(None, 'lat', 'lon')
- slabs: float32 [512, 64, 1536], P(('lat', 'lon'))
Inputs may be any that keep to these rules, and one draw needn't show every extreme that they name: owner_device[s, 0] numbers a device along the joined axes lat+lon; no device owns more than 4 level-variables, one owns exactly 4, and every device owns at least one.
All inputs are finite; a program needn't handle non-finite values.
Results may differ from a plain program's by a relative error of at most 0.0003.
Values sent between devices are 32-bit elements; how exact they have to be, the bound alone decides.
A program may use at most 64 MiB of HBM per device.

v0:
```python
import math
import jax
import jax.numpy as jnp
from jax import lax
from jax.sharding import PartitionSpec as P

NLAT_GLOBE = 768
HIGH_ACCURACY = lax.Precision.HIGHEST


def padded(block, sides, width, periodic):
    for axis, dim in sides:
        count = lax.axis_size(axis)
        forward = [(i, i + 1) for i in range(count - 1)]
        if periodic:
            forward.append((count - 1, 0))
        backward = [(target, source) for source, target in forward]
        low = lax.ppermute(
            lax.slice_in_dim(block, block.shape[dim] - width, None, axis=dim), axis, forward
        )
        high = lax.ppermute(lax.slice_in_dim(block, 0, width, axis=dim), axis, backward)
        block = jnp.concatenate([low, block, high], axis=dim)
    return block


def slot_sources(owner_device, devices_all, most_slots):
    owners = owner_device[:, 0]
    level_ids = jnp.arange(owners.shape[0], dtype=jnp.int32)
    sharing = (owners[:, None] == owners[None, :]) & (level_ids[None, :] < level_ids[:, None])
    rank_in = jnp.sum(sharing.astype(jnp.int32), axis=1)
    slot_of = owners * most_slots + rank_in
    slot_numbers = jnp.arange(devices_all * most_slots, dtype=jnp.int32)
    matches = slot_of[None, :] == slot_numbers[:, None]
    filled = jnp.any(matches, axis=1)
    source = jnp.argmax(matches.astype(jnp.int32), axis=1)
    return (owners, rank_in, source, filled)


def rate_tables(inverse, block_len):
    slab_total, length = inverse.shape
    blocks = length // block_len
    decays = jnp.exp(-inverse)
    weights = jnp.sqrt(1.0 - decays * decays).reshape(slab_total, blocks, block_len)
    logsum = jnp.cumsum(-inverse.reshape(slab_total, blocks, block_len), axis=2)
    within = jnp.arange(block_len)
    below = within[:, None] >= within[None, :]
    spread = jnp.minimum(logsum[:, :, :, None] - logsum[:, :, None, :], 0.0)
    transfer = jnp.where(below, jnp.exp(spread), 0.0) * weights[:, :, None, :]
    return (transfer, jnp.exp(logsum))


def block_carries(gains, ends):

    def advance(running, inputs):
        gain, tail = inputs
        return (gain[:, None] * running + tail, running)

    initial = jnp.zeros_like(ends[:, 0])
    _, entries = lax.scan(advance, initial, (gains.T, jnp.moveaxis(ends, 1, 0)))
    return jnp.moveaxis(entries, 0, 1)


def sweep_rows(fields, transfer, reach):
    slab_total, length, across = fields.shape
    blocks, block_len = (reach.shape[1], reach.shape[2])
    parts = fields.reshape(slab_total, blocks, block_len, across)
    local = jnp.einsum("sbnm,sbmw->sbnw", transfer, parts, precision=HIGH_ACCURACY)
    entries = block_carries(reach[:, :, -1], local[:, :, -1, :])
    result = local + reach[:, :, :, None] * entries[:, :, None, :]
    return result.reshape(slab_total, length, across)


def sweep_cols(fields, transfer, reach):
    slab_total, across, length = fields.shape
    blocks, block_len = (reach.shape[1], reach.shape[2])
    parts = fields.reshape(slab_total, across, blocks, block_len)
    local = jnp.einsum("sbnm,swbm->swbn", transfer, parts, precision=HIGH_ACCURACY)
    entries = block_carries(reach[:, :, -1], jnp.swapaxes(local[:, :, :, -1], 1, 2))
    result = local + reach[:, None, :, :] * jnp.swapaxes(entries, 1, 2)[:, :, :, None]
    return result.reshape(slab_total, across, length)


def filter_slabs(slab, lat_inverse, lon_inverse):
    slot_total, lat_full, lon_full = slab.shape
    lat_block = math.gcd(lat_full, 128)
    lat_mats, lat_reach = rate_tables(lat_inverse, lat_block)
    northward = sweep_rows(slab, lat_mats, lat_reach)
    back_mats, back_reach = rate_tables(jnp.flip(lat_inverse, 1), lat_block)
    southward = jnp.flip(sweep_rows(jnp.flip(northward, 1), back_mats, back_reach), 1)
    lon_block = math.gcd(lon_full, 128)
    lon_table = jnp.broadcast_to(lon_inverse[:, None], (slot_total, lon_full))
    lon_mats, lon_reach = rate_tables(lon_table, lon_block)
    places = jnp.arange(lon_full, dtype=jnp.float32)
    closing = 1.0 / (1.0 - jnp.exp(-lon_full * lon_inverse))
    eastward = sweep_cols(southward, lon_mats, lon_reach)
    eastward = eastward + jnp.exp(-(places[None, :] + 1.0) * lon_inverse[:, None])[:, None, :] * (
        eastward[:, :, -1:] * closing[:, None, None]
    )
    westward = jnp.flip(sweep_cols(jnp.flip(eastward, 2), lon_mats, lon_reach), 2)
    westward = westward + jnp.exp(-(lon_full - places[None, :]) * lon_inverse[:, None])[
        :, None, :
    ] * (westward[:, :, :1] * closing[:, None, None])
    return westward


def to_owners(columns, source, filled, most_slots, lat_count, lon_count):
    level_vars, latitude_points, longitude_points = columns.shape
    devices_all = lat_count * lon_count
    by_slot = source.reshape(devices_all, most_slots).T.reshape(-1)
    live_slot = filled.reshape(devices_all, most_slots).T.reshape(-1)
    packed = jnp.where(live_slot[:, None, None], jnp.take(columns, by_slot, axis=0), 0.0)
    moved = lax.all_to_all(
        packed.reshape(most_slots, devices_all, latitude_points, longitude_points),
        ("lat", "lon"),
        split_axis=1,
        concat_axis=1,
        tiled=True,
    )
    moved = moved.reshape(most_slots, lat_count, lon_count, latitude_points, longitude_points)
    return moved.transpose(0, 1, 3, 2, 4).reshape(
        most_slots, lat_count * latitude_points, lon_count * longitude_points
    )


def into_columns(slab, owners, rank_in, lat_count, lon_count, latitude_points, longitude_points):
    most_slots = slab.shape[0]
    devices_all = lat_count * lon_count
    pieces = slab.reshape(
        most_slots, lat_count, latitude_points, lon_count, longitude_points
    ).transpose(0, 1, 3, 2, 4)
    returned = lax.all_to_all(
        pieces.reshape(most_slots, devices_all, latitude_points, longitude_points),
        ("lat", "lon"),
        split_axis=1,
        concat_axis=1,
        tiled=True,
    )
    flat_slots = returned.reshape(most_slots * devices_all, latitude_points, longitude_points)
    return jnp.take(flat_slots, rank_in * devices_all + owners, axis=0)


def winds_from(filtered, lat_pos, lat_full):
    level_vars, latitude_points, longitude_points = filtered.shape
    level_count_total = level_vars // 2
    lat_ext = padded(filtered, (("lat", 1),), 1, False)
    lon_ext = padded(filtered, (("lon", 2),), 1, True)
    d_lat = (lat_ext[:, 2:, :] - lat_ext[:, :-2, :]) * 0.5
    d_lon = (lon_ext[:, :, 2:] - lon_ext[:, :, :-2]) * 0.5
    latitude_rows = (lat_pos * latitude_points + jnp.arange(latitude_points)).astype(
        jnp.float32
    ) + float(NLAT_GLOBE - lat_full)
    latitude = jnp.pi * ((latitude_rows + 0.5) / NLAT_GLOBE - 0.5)
    metric = (1.0 / jnp.maximum(jnp.cos(latitude), 0.2))[None, :, None]
    east_wind = -d_lat[:level_count_total] + d_lon[level_count_total:] * metric
    north_wind = d_lon[:level_count_total] * metric + d_lat[level_count_total:]
    return jnp.concatenate([east_wind, north_wind], axis=0)


def shards(control, vert_band, lat_length, lon_length, band_index, owner_device):
    level_vars, latitude_points, longitude_points = control.shape
    lat_count = lax.axis_size("lat")
    lon_count = lax.axis_size("lon")
    devices_all = lat_count * lon_count
    most_slots = 2 * ((level_vars + devices_all - 1) // devices_all)
    lat_full = latitude_points * lat_count
    lat_pos = lax.axis_index("lat")
    lon_pos = lax.axis_index("lon")
    my_device = lat_pos * lon_count + lon_pos
    level_count_total = level_vars // 2
    band_width = vert_band.shape[1]
    half_band = band_width // 2
    diagonals = jnp.stack(
        [
            jnp.eye(level_count_total, k=offset - half_band, dtype=jnp.float32)
            for offset in range(band_width)
        ]
    )
    band_matrices = jnp.eye(level_count_total, dtype=jnp.float32)[None] + jnp.einsum(
        "vok,okl->vkl", vert_band, diagonals, precision=HIGH_ACCURACY
    )
    mixed = jnp.einsum(
        "jme,jet->jmt",
        band_matrices,
        control.reshape(2, level_count_total, latitude_points * longitude_points),
        precision=HIGH_ACCURACY,
    )
    mixed = mixed.reshape(level_vars, latitude_points, longitude_points)
    band_onehot = (
        band_index[None, :] == jnp.arange(lat_length.shape[1], dtype=jnp.int32)[:, None]
    ).astype(jnp.float32)
    lat_inverse = 1.0 / jnp.dot(lat_length, band_onehot, precision=HIGH_ACCURACY)
    lon_inverse = 1.0 / lon_length
    owners, rank_in, source, filled = slot_sources(owner_device, devices_all, most_slots)
    slab = to_owners(mixed, source, filled, most_slots, lat_count, lon_count)
    my_sources = lax.dynamic_slice_in_dim(source, my_device * most_slots, most_slots)
    slab_lat = jnp.take(lat_inverse, my_sources, axis=0)
    slab_lon = jnp.take(lon_inverse, my_sources, axis=0)
    slabs = filter_slabs(slab, slab_lat, slab_lon)
    filtered = into_columns(
        slabs, owners, rank_in, lat_count, lon_count, latitude_points, longitude_points
    )
    winds = winds_from(filtered, lat_pos, lat_full)
    return (winds, slabs)


def solution(mesh):
    placed = (P(None, "lat", "lon"), P(), P(), P(), P(), P())
    return jax.shard_map(
        shards,
        mesh=mesh,
        in_specs=placed,
        out_specs=(P(None, "lat", "lon"), P(("lat", "lon"), None, None)),
        check_vma=False,
    )
```

profile of v0, /device:TPU:1, one launch (start us, length us, event | category | flops | bytes accessed | tf_op | source)
XLA Modules:
  0.0 158.4 jit_solution(12169647411586467668)
XLA Ops:
  0.7 0.9 convert_reduce_fusion
  5.0 1.7 %reshape.571 = f32[2,127,768]{1,0,2:T(2,128)S(1)} reshape(f32[254,8,96]{0,2,1:T(8,128)} %param.10) | data formatting | bytes 1560576 | tf_op jit(solution)/shard_map/reshape | solution.py:184
  7.7 2.8 %stack.5 = pred[9,127,127]{2,0,1:T(8,128)(4,1)S(1)} concatenate(pred[1,127,127]{2,0,1:T(4,128)(4,1)S(1)} %iota_compare_fusion.12, pred[1,127,127]{2,0,1:T(4,128)(4,1)S(1)} %get-tuple-element.235, pred[1,127,127]{2,0,1:T(4,128)(4,1)S(1)} %get-tuple-element.234, pred[1,127,127]{2,0,1:T(4,128)(4,1)S(1)} %get-tuple-element.233, pred[1,127,127]{2,0,1:T(4,128)(4,1)S(1)} %get-tuple-element.232, ...), dimensions={0} | concatenate | bytes 290322 | tf_op jit(solution)/shard_map/stack | solution.py:172
  12.5 1.9 %gather_fusion.1 = f32[512,8,96]{2,1,0:T(8,128)S(1)} fusion(f32[254,8,96]{2,1,0:T(8,128)S(1)} %reshape.618, s32[1024]{0:T(1024)S(1)} %pad_clamp_fusion.1), kind=kCustom, calls=%fused_computation.1 | custom fusion | bytes 3147776 | tf_op jit(solution)/shard_map/jit(_take)/gather | solution.py:111
  14.4 2.7 %fusion.4 = f32[4,128,8,96]{3,2,0,1:T(8,128)} fusion(f32[4,128,8,96]{3,2,1,0:T(8,128)S(1)} %bitcast.98, pred[4,128]{0,1:T(8,128)(4,1)S(1)} %compare_and_fusion, pred[4,128]{0,1:T(8,128)(4,1)S(1)} %bitcast.104), kind=kLoop, calls=%fused_computation.18 | loop fusion | flops 786432 | bytes 3146752 | tf_op jit(solution)/shard_map/jit(_where)/select_n | solution.py:111
  17.0 11.5 %all-to-all-start = ((f32[4,128,8,96]{3,2,0,1:T(8,128)}), f32[4,128,8,96]{3,2,0,1:T(8,128)S(1)}, u32[]{:S(2)}, u32[]{:S(2)}) async-start(f32[4,128,8,96]{3,2,0,1:T(8,128)} %fusion.4), calls=%async_computation | async-start | bytes 4194304 | tf_op jit(solution)/shard_map/all_to_all | solution.py:112
  30.5 1.1 reduce_window_sum.30
  32.6 25.6 %all-to-all-done = f32[4,128,8,96]{3,2,0,1:T(8,128)S(1)} async-done(((f32[4,128,8,96]{3,2,0,1:T(8,128)}), f32[4,128,8,96]{3,2,0,1:T(8,128)S(1)}, u32[]{:S(2)}, u32[]{:S(2)}) %all-to-all-start) | async-done | bytes 1572896 | tf_op jit(solution)/shard_map/all_to_all | solution.py:112
  58.2 1.3 copy-done.1
  59.6 2.8 %copy.100 = f32[4,8,8,16,96]{4,3,2,1,0:T(8,128)S(1)} copy(f32[4,8,8,16,96]{4,2,0,3,1:T(8,128)} %bitcast.97) | data formatting | bytes 3145728 | tf_op jit(solution)/shard_map/transpose | solution.py:120
  62.4 2.1 %reshape.575 = f32[4,64,1536]{2,1,0:T(8,128)} reshape(f32[4,8,8,16,96]{4,3,2,1,0:T(8,128)S(1)} %copy.100) | data formatting | bytes 3145728 | tf_op jit(solution)/shard_map/reshape.12
  64.5 2.9 %convolution_add_fusion.1 = f32[4,64,1536]{2,1,0:T(8,128)S(1)} fusion(f32[4,64,1536]{2,1,0:T(8,128)} %reshape.575, f32[4,64]{1,0:T(4,128)S(1)} %exponential_multiply_fusion.1, f32[4,64]{1,0:T(4,128)S(1)} %get-tuple-element.208, f32[4,64]{1,0:T(4,128)S(1)} %reduce_window_sum.29, pred[64,64]{1,0:T(8,128)(4,1)S(1)} %iota_compare_fusion.13), kind=kOutput, calls=%fused_computation.16 | convolution fusion | flops 302448640 | bytes 3152896 | tf_op jit(solution)/shard_map/sbnm,sbmw->sbnw/dot_general | solution.py:67
  67.9 1.5 convolution_add_fusion
  69.5 4.2 %reverse.8 = f32[4,64,1536]{2,1,0:T(8,128)} reverse(f32[4,64,1536]{2,1,0:T(8,128)S(1)} %convolution_add_fusion), dimensions={1} | reverse | bytes 3145728 | tf_op jit(solution)/shard_map/reverse.2
  73.6 7.6 %fusion.19 = f32[4,64,12,128]{3,1,2,0:T(8,128)S(1)} fusion(f32[4]{0:T(128)S(1)} %get-tuple-element.227, f32[4,12,128]{2,1,0:T(8,128)S(1)} %reduce_window_sum.30, pred[128,128]{1,0:T(8,128)(4,1)S(1)} %iota_compare_fusion.2, f32[4,64,1536]{2,1,0:T(8,128)} %reverse.8), kind=kOutput, calls=%fused_computation.39 | convolution fusion | flops 607125504 | bytes 3186704 | tf_op jit(solution)/shard_map/sbnm,swbm->swbn/dot_general | solution.py:77
  82.2 1.4 while.6
  84.8 1.4 rev.15
  86.3 6.2 %fusion.22 = f32[4,64,12,128]{3,1,2,0:T(8,128)S(1)} fusion(f32[4]{0:T(128)S(1)} %get-tuple-element.227, f32[4,12,128]{2,1,0:T(8,128)S(1)} %reduce_window_sum.30, pred[128,128]{1,0:T(8,128)(4,1)S(1)} %iota_compare_fusion.2, f32[4,64,1536]{2,1,0:T(8,128)S(1)} %rev.15), kind=kOutput, calls=%fused_computation.40 | convolution fusion | flops 607125504 | bytes 3186704 | tf_op jit(solution)/shard_map/sbnm,swbm->swbn/dot_general | solution.py:77
  93.5 1.2 while.7
  95.4 1.4 rev.16
  96.8 1.4 multiply_add_fusion
  98.2 1.9 %reshape.581 = f32[4,8,8,16,96]{4,3,2,1,0:T(8,128)S(1)} reshape(f32[4,64,1536]{2,1,0:T(8,128)} %multiply_add_fusion) | data formatting | bytes 3145728 | tf_op jit(solution)/shard_map/reshape | solution.py:128
  101.0 1.6 %copy.112 = f32[4,128,8,96]{3,2,0,1:T(8,128)} copy(f32[4,128,8,96]{3,2,1,0:T(8,128)S(1)} %bitcast.99) | data formatting | bytes 3145728 | tf_op jit(solution)/shard_map/reshape | solution.py:132
  102.6 4.8 %all-to-all-start.1 = ((f32[4,128,8,96]{3,2,0,1:T(8,128)}), f32[4,128,8,96]{3,2,0,1:T(8,128)S(1)}, u32[]{:S(2)}, u32[]{:S(2)}) async-start(f32[4,128,8,96]{3,2,0,1:T(8,128)} %copy.112), calls=%async_computation.1 | async-start | bytes 4194304 | tf_op jit(solution)/shard_map/all_to_all | solution.py:131
  107.5 29.7 %all-to-all-done.1 = f32[4,128,8,96]{3,2,0,1:T(8,128)S(1)} async-done(((f32[4,128,8,96]{3,2,0,1:T(8,128)}), f32[4,128,8,96]{3,2,0,1:T(8,128)S(1)}, u32[]{:S(2)}, u32[]{:S(2)}) %all-to-all-start.1) | async-done | bytes 1572896 | tf_op jit(solution)/shard_map/all_to_all | solution.py:131
  137.2 1.5 copy.113
  138.7 2.3 %gather_fusion.3 = f32[254,8,96]{2,1,0:T(8,128)S(1)} fusion(f32[512,8,96]{2,1,0:T(8,128)} %bitcast.100, s32[1024]{0:T(1024)S(1)} %pad_clamp_fusion), kind=kCustom, calls=%fused_computation.3 | custom fusion | bytes 1561592 | tf_op jit(solution)/shard_map/jit(_take)/gather | solution.py:139
  142.5 3.1 %collective-permute-start = (f32[254,1,96]{2,1,0:T(1,128)}, f32[254,1,96]{2,1,0:T(1,128)S(1)}, u32[]{:S(2)}, u32[]{:S(2)}) collective-permute-start(f32[254,1,96]{2,1,0:T(1,128)} %get-tuple-element.218), channel_id=1, source_target_pairs={{16,0},{32,16},{48,32},{64,48},{80,64},{96,80},{112,96},{17,1},{33... | collective-permute-start | bytes 292616 | tf_op jit(solution)/shard_map/ppermute | solution.py:21
  145.6 2.5 %collective-permute-start.1 = (f32[254,1,96]{2,1,0:T(1,128)S(1)}, f32[254,1,96]{2,1,0:T(1,128)S(1)}, u32[]{:S(2)}, u32[]{:S(2)}) collective-permute-start(f32[254,1,96]{2,1,0:T(1,128)S(1)} %get-tuple-element.219), channel_id=1, source_target_pairs={{0,16},{16,32},{32,48},{48,64},{64,80},{80,96},{96,112},{1,17},{17... | collective-permute-start | bytes 292616 | tf_op jit(solution)/shard_map/ppermute | solution.py:18
  149.4 4.3 %collective-permute-start.2 = (f32[254,8,1]{0,1,2:T(8,128)S(1)}, f32[254,8,1]{0,1,2:T(8,128)S(1)}, u32[]{:S(2)}, u32[]{:S(2)}) collective-permute-start(f32[254,8,1]{0,1,2:T(8,128)S(1)} %copy.114), channel_id=1, source_target_pairs={{1,0},{2,1},{3,2},{4,3},{5,4},{6,5},{7,6},{8,7},{9,8},{10,9},{11,1... | collective-permute-start | bytes 24392 | tf_op jit(solution)/shard_map/ppermute | solution.py:21
  155.5 1.4 fusion.28
  157.2 1.3 copy.118
  (167 shorter events, 21.5 us)
Async XLA Ops:
  0.6 28.0 %copy-start = (f32[254,8]{0,1:T(8,128)S(1)}, f32[254,8]{0,1:T(8,128)}, u32[]{:S(2)}) copy-start(f32[254,8]{0,1:T(8,128)} %param.12) | copy-start | bytes 24388
  17.0 11.6 %copy-start.4 = (s32[64]{0:T(128)S(1)}, s32[64]{0:T(128)}, u32[]{:S(2)}) copy-start(s32[64]{0:T(128)} %param.14) | copy-start | bytes 772
  17.0 12.7 %copy-start.3 = (f32[254]{0:T(256)S(1)}, f32[254]{0:T(256)}, u32[]{:S(2)}) copy-start(f32[254]{0:T(256)} %param.13) | copy-start | bytes 3052
  17.0 41.2 %all-to-all-start = ((f32[4,128,8,96]{3,2,0,1:T(8,128)}), f32[4,128,8,96]{3,2,0,1:T(8,128)S(1)}, u32[]{:S(2)}, u32[]{:S(2)}) async-start(f32[4,128,8,96]{3,2,0,1:T(8,128)} %fusion.4), calls=%async_computation | async-start | bytes 4194304 | tf_op jit(solution)/shard_map/all_to_all | solution.py:112
  58.2 1.4 copy-start.1
  102.6 4.8 %copy-start.2 = (s32[254,1]{0,1:T(1,128)S(1)}, s32[254,1]{0,1:T(1,128)}, u32[]{:S(2)}) copy-start(s32[254,1]{0,1:T(1,128)} %param.15) | copy-start | bytes 3052
  102.6 34.6 %all-to-all-start.1 = ((f32[4,128,8,96]{3,2,0,1:T(8,128)}), f32[4,128,8,96]{3,2,0,1:T(8,128)S(1)}, u32[]{:S(2)}, u32[]{:S(2)}) async-start(f32[4,128,8,96]{3,2,0,1:T(8,128)} %copy.112), calls=%async_computation.1 | async-start | bytes 4194304 | tf_op jit(solution)/shard_map/all_to_all | solution.py:131
  142.5 12.9 %collective-permute-start = (f32[254,1,96]{2,1,0:T(1,128)}, f32[254,1,96]{2,1,0:T(1,128)S(1)}, u32[]{:S(2)}, u32[]{:S(2)}) collective-permute-start(f32[254,1,96]{2,1,0:T(1,128)} %get-tuple-element.218), channel_id=1, source_target_pairs={{16,0},{32,16},{48,32},{64,48},{80,64},{96,80},{112,96},{17,1},{33... | collective-permute-start | bytes 292616 | tf_op jit(solution)/shard_map/ppermute | solution.py:21
  145.6 9.9 %collective-permute-start.1 = (f32[254,1,96]{2,1,0:T(1,128)S(1)}, f32[254,1,96]{2,1,0:T(1,128)S(1)}, u32[]{:S(2)}, u32[]{:S(2)}) collective-permute-start(f32[254,1,96]{2,1,0:T(1,128)S(1)} %get-tuple-element.219), channel_id=1, source_target_pairs={{0,16},{16,32},{32,48},{48,64},{64,80},{80,96},{96,112},{1,17},{17... | collective-permute-start | bytes 292616 | tf_op jit(solution)/shard_map/ppermute | solution.py:18
  148.9 6.1 %collective-permute-start.3 = (f32[254,8,1]{0,1,2:T(8,128)S(1)}, f32[254,8,1]{0,1,2:T(8,128)S(1)}, u32[]{:S(2)}, u32[]{:S(2)}) collective-permute-start(f32[254,8,1]{0,1,2:T(8,128)S(1)} %copy.116), channel_id=1, source_target_pairs={{0,1},{1,2},{2,3},{3,4},{4,5},{5,6},{6,7},{7,8},{8,9},{9,10},{10,1... | collective-permute-start | bytes 24392 | tf_op jit(solution)/shard_map/ppermute | solution.py:18
  149.4 5.1 %collective-permute-start.2 = (f32[254,8,1]{0,1,2:T(8,128)S(1)}, f32[254,8,1]{0,1,2:T(8,128)S(1)}, u32[]{:S(2)}, u32[]{:S(2)}) collective-permute-start(f32[254,8,1]{0,1,2:T(8,128)S(1)} %copy.114), channel_id=1, source_target_pairs={{1,0},{2,1},{3,2},{4,3},{5,4},{6,5},{7,6},{8,7},{9,8},{10,9},{11,1... | collective-permute-start | bytes 24392 | tf_op jit(solution)/shard_map/ppermute | solution.py:21
where the time goes:
time: 159 us; the launch traced here: 158 us
  waiting for transfers between devices  56.1 us (35%)
  local copies, waits for them, and re-layouts  38.1 us (24%)
  starting transfers between devices  26.6 us (17%)
  matrix products  19.9 us (13%)
  other arithmetic  16.3 us (10%)
    all_to_all x1, waiting for transfers between devices, into_columns(): lax.all_to_all(pieces.reshape(most_slots, devices_all, latitude_points, l...  29.7 us
    all_to_all x1, waiting for transfers between devices, to_owners(): lax.all_to_all(packed.reshape(most_slots, devices_all, latitude_points, l...  25.6 us
    dot_general x2, matrix products, sweep_cols(): jnp.einsum('sbnm,swbm->swbn', transfer, parts, precision=HIGH_ACCURACY)  13.8 us
    all_to_all x1, starting transfers between devices, to_owners(): lax.all_to_all(packed.reshape(most_slots, devices_all, latitude_points, l...  11.5 us
    ppermute x2, starting transfers between devices, padded(): lax.ppermute(lax.slice_in_dim(block, 0, width, axis=dim), axis, backward)  7.38 us
    another operation x5, local copies, waits for them, and re-layouts  6.81 us
    all_to_all x1, starting transfers between devices, into_columns(): lax.all_to_all(pieces.reshape(most_slots, devices_all, latitude_points, l...  4.75 us
    dot_general x2, matrix products, sweep_rows(): jnp.einsum('sbnm,sbmw->sbnw', transfer, parts, precision=HIGH_ACCURACY)  4.42 us
  transfers between devices with their start and end apart: 6, of which 3 were waited for; matrix products, arithmetic and copies ran while one was open for 4% of the time, Pallas kernels for 0%

commit v1 on v0

--- a/solution.py
+++ b/solution.py
@@ -1,3 +1,4 @@
+import functools
 import math
 import jax
 import jax.numpy as jnp
@@ -6,6 +7,17 @@
 
 NLAT_GLOBE = 768
 HIGH_ACCURACY = lax.Precision.HIGHEST
+
+
+def step_on_seats_all(u_in, net_axis):
+    main = lax.psum(1, net_axis)
+    value_now = jnp.split(u_in, main, 1)
+    state_now = jnp.stack(value_now)
+    known = lax.all_to_all(state_now, net_axis, split_axis=0, concat_axis=0)
+    return jnp.concatenate(known, 1)
+
+
+views_lead = functools.partial(step_on_seats_all, net_axis=("lat", "lon"))
 
 
 def padded(block, sides, width, periodic):
@@ -109,13 +121,7 @@
     by_slot = source.reshape(devices_all, most_slots).T.reshape(-1)
     live_slot = filled.reshape(devices_all, most_slots).T.reshape(-1)
     packed = jnp.where(live_slot[:, None, None], jnp.take(columns, by_slot, axis=0), 0.0)
-    moved = lax.all_to_all(
-        packed.reshape(most_slots, devices_all, latitude_points, longitude_points),
-        ("lat", "lon"),
-        split_axis=1,
-        concat_axis=1,
-        tiled=True,
-    )
+    moved = views_lead(packed.reshape(most_slots, devices_all, latitude_points, longitude_points))
     moved = moved.reshape(most_slots, lat_count, lon_count, latitude_points, longitude_points)
     return moved.transpose(0, 1, 3, 2, 4).reshape(
         most_slots, lat_count * latitude_points, lon_count * longitude_points

time: 159 us -> 239 us (1.50)
  local copies, waits for them, and re-layouts: 38.1 us -> 118 us
    unnamed x13 -> x140, local copies, waits for them, and re-layouts: 3.57 us -> 79.8 us
    rev x1, local copies, waits for them, and re-layouts: 1.45 us -> 4.78 us  [filter_slabs(): jnp.flip(eastward, 2)]
    another operation x5 -> x6, local copies, waits for them, and re-layouts: 6.81 us -> 7.42 us
  transfers between devices with their start and end apart: 6 -> 6, of which waited for: 3 -> 3; matrix products, arithmetic and copies ran while one was open for 4% -> 2% of each run, Pallas kernels for 0% -> 0%
where the time goes in v1:
time: 239 us
  local copies, waits for them, and re-layouts  118 us (49%)
  waiting for transfers between devices  56.2 us (24%)
  starting transfers between devices  26.6 us (11%)
  matrix products  21.3 us (9%)
  other arithmetic  14.7 us (6%)
    unnamed x140, local copies, waits for them, and re-layouts  79.8 us
    all_to_all x1, waiting for transfers between devices, into_columns(): lax.all_to_all(pieces.reshape(most_slots, devices_all, latitude_points, l...  29.7 us
    all_to_all x1, waiting for transfers between devices, step_on_seats_all(): known = lax.all_to_all(state_now, net_axis, split_axis=0, concat_axis=0)  25.7 us
    dot_general x2, matrix products, sweep_cols(): jnp.einsum('sbnm,swbm->swbn', transfer, parts, precision=HIGH_ACCURACY)  15.1 us
    all_to_all x1, starting transfers between devices, step_on_seats_all(): known = lax.all_to_all(state_now, net_axis, split_axis=0, concat_axis=0)  11.5 us
    ppermute x2, starting transfers between devices, padded(): lax.ppermute(lax.slice_in_dim(block, 0, width, axis=dim), axis, backward)  7.38 us
    another operation x5, local copies, waits for them, and re-layouts  6.81 us
  transfers between devices with their start and end apart: 6, of which 3 were waited for; matrix products, arithmetic and copies ran while one was open for 2% of the time, Pallas kernels for 0%

profile of v1, /device:TPU:1, one launch (start us, length us, event | category | flops | bytes accessed | tf_op | source)
XLA Modules:
  0.0 238.6 jit_solution(17321922456233702022)
XLA Ops:
  0.7 0.9 convert_reduce_fusion
  5.1 1.7 reshape.571
  7.8 2.8 %stack.402 = pred[9,127,127]{2,0,1:T(8,128)(4,1)S(1)} concatenate(pred[1,127,127]{2,0,1:T(4,128)(4,1)S(1)} %iota_compare_fusion.12, pred[1,127,127]{2,0,1:T(4,128)(4,1)S(1)} %get-tuple-element.237, pred[1,127,127]{2,0,1:T(4,128)(4,1)S(1)} %get-tuple-element.236, pred[1,127,127]{2,0,1:T(4,128)(4,1)S(1)} %get-tuple-element.235, pred[1,127,127]{2,0,1:T(4,128)(4,1)S(1)} %get-tuple-element.234, ...), dimensions={0} | concatenate | bytes 290322 | tf_op jit(solution)/shard_map/stack | solution.py:178
  12.6 1.9 gather_fusion.1
  14.5 1.1 fusion.4
  92.5 11.5 %all-to-all-start = ((f32[128,4,1,8,96]{4,3,1,2,0:T(8,128)}), f32[128,4,1,8,96]{4,3,1,2,0:T(8,128)S(1)}, u32[]{:S(2)}, u32[]{:S(2)}) async-start(f32[128,4,1,8,96]{4,3,1,2,0:T(8,128)} %constant_dynamic-update-slice_fusion), calls=%async_computation | async-start | bytes 4194304 | tf_op jit(solution)/shard_map/all_to_all | solution.py:16
  105.9 1.1 reduce_window_sum.30
  108.0 25.7 %all-to-all-done = f32[128,4,1,8,96]{4,3,1,2,0:T(8,128)S(1)} async-done(((f32[128,4,1,8,96]{4,3,1,2,0:T(8,128)}), f32[128,4,1,8,96]{4,3,1,2,0:T(8,128)S(1)}, u32[]{:S(2)}, u32[]{:S(2)}) %all-to-all-start) | async-done | bytes 1572896 | tf_op jit(solution)/shard_map/all_to_all | solution.py:16
  133.7 1.3 copy-done.1
  135.0 2.8 %copy.354 = f32[4,8,8,16,96]{4,3,2,1,0:T(8,128)S(1)} copy(f32[4,8,8,16,96]{4,2,0,3,1:T(8,128)} %bitcast.611) | data formatting | bytes 3145728 | tf_op jit(solution)/shard_map/transpose | solution.py:126
  137.9 2.1 reshape.575
  140.0 2.9 %convolution_add_fusion.1 = f32[4,64,1536]{2,1,0:T(8,128)S(1)} fusion(f32[4,64,1536]{2,1,0:T(8,128)} %reshape.575, f32[4,64]{1,0:T(4,128)S(1)} %exponential_multiply_fusion.1, f32[4,64]{1,0:T(4,128)S(1)} %get-tuple-element.208, f32[4,64]{1,0:T(4,128)S(1)} %reduce_window_sum.29, pred[64,64]{1,0:T(8,128)(4,1)S(1)} %iota_compare_fusion.13), kind=kOutput, calls=%fused_computation.16 | convolution fusion | flops 302448640 | bytes 3152896 | tf_op jit(solution)/shard_map/sbnm,sbmw->sbnw/dot_general | solution.py:79
  143.4 1.5 convolution_add_fusion
  144.9 4.2 %reverse.8 = f32[4,64,1536]{2,1,0:T(8,128)} reverse(f32[4,64,1536]{2,1,0:T(8,128)S(1)} %convolution_add_fusion), dimensions={1} | reverse | bytes 3145728 | tf_op jit(solution)/shard_map/reverse.2
  149.1 7.6 %fusion.19 = f32[4,64,12,128]{3,1,2,0:T(8,128)S(1)} fusion(f32[4]{0:T(128)S(1)} %get-tuple-element.227, f32[4,12,128]{2,1,0:T(8,128)S(1)} %reduce_window_sum.30, pred[128,128]{1,0:T(8,128)(4,1)S(1)} %iota_compare_fusion.2, f32[4,64,1536]{2,1,0:T(8,128)} %reverse.8), kind=kOutput, calls=%fused_computation.39 | convolution fusion | flops 607125504 | bytes 3186704 | tf_op jit(solution)/shard_map/sbnm,swbm->swbn/dot_general | solution.py:89
  157.7 1.4 while.6
  160.3 4.8 %rev.15 = f32[4,64,1536]{2,1,0:T(8,128)} reverse(f32[4,64,1536]{2,1,0:T(8,128)S(1)} %multiply_add_fusion.1), dimensions={2} | reverse | bytes 3145728 | tf_op jit(solution)/shard_map/jit(_flip)/rev | solution.py:111
  165.1 7.6 %fusion.22 = f32[4,64,12,128]{3,1,2,0:T(8,128)S(1)} fusion(f32[4]{0:T(128)S(1)} %get-tuple-element.227, f32[4,12,128]{2,1,0:T(8,128)S(1)} %reduce_window_sum.30, pred[128,128]{1,0:T(8,128)(4,1)S(1)} %iota_compare_fusion.2, f32[4,64,1536]{2,1,0:T(8,128)} %rev.15), kind=kOutput, calls=%fused_computation.40 | convolution fusion | flops 607125504 | bytes 3186704 | tf_op jit(solution)/shard_map/sbnm,swbm->swbn/dot_general | solution.py:89
  173.7 1.2 while.7
  175.5 1.4 rev.16
  177.0 1.4 multiply_add_fusion
  178.3 1.9 reshape.581
  181.2 1.6 copy.366
  182.8 4.8 %all-to-all-start.1 = ((f32[4,128,8,96]{3,2,0,1:T(8,128)}), f32[4,128,8,96]{3,2,0,1:T(8,128)S(1)}, u32[]{:S(2)}, u32[]{:S(2)}) async-start(f32[4,128,8,96]{3,2,0,1:T(8,128)} %copy.366), calls=%async_computation.1 | async-start | bytes 4194304 | tf_op jit(solution)/shard_map/all_to_all | solution.py:137
  187.6 29.7 %all-to-all-done.1 = f32[4,128,8,96]{3,2,0,1:T(8,128)S(1)} async-done(((f32[4,128,8,96]{3,2,0,1:T(8,128)}), f32[4,128,8,96]{3,2,0,1:T(8,128)S(1)}, u32[]{:S(2)}, u32[]{:S(2)}) %all-to-all-start.1) | async-done | bytes 1572896 | tf_op jit(solution)/shard_map/all_to_all | solution.py:137
  217.4 1.5 copy.367
  218.9 2.3 gather_fusion.3
  222.7 3.1 %collective-permute-start = (f32[254,1,96]{2,1,0:T(1,128)}, f32[254,1,96]{2,1,0:T(1,128)S(1)}, u32[]{:S(2)}, u32[]{:S(2)}) collective-permute-start(f32[254,1,96]{2,1,0:T(1,128)} %get-tuple-element.218), channel_id=1, source_target_pairs={{16,0},{32,16},{48,32},{64,48},{80,64},{96,80},{112,96},{17,1},{33... | collective-permute-start | bytes 292616 | tf_op jit(solution)/shard_map/ppermute | solution.py:33
  225.8 2.5 %collective-permute-start.1 = (f32[254,1,96]{2,1,0:T(1,128)S(1)}, f32[254,1,96]{2,1,0:T(1,128)S(1)}, u32[]{:S(2)}, u32[]{:S(2)}) collective-permute-start(f32[254,1,96]{2,1,0:T(1,128)S(1)} %get-tuple-element.219), channel_id=1, source_target_pairs={{0,16},{16,32},{32,48},{48,64},{64,80},{80,96},{96,112},{1,17},{17... | collective-permute-start | bytes 292616 | tf_op jit(solution)/shard_map/ppermute | solution.py:30
  229.6 4.3 %collective-permute-start.2 = (f32[254,8,1]{0,1,2:T(8,128)S(1)}, f32[254,8,1]{0,1,2:T(8,128)S(1)}, u32[]{:S(2)}, u32[]{:S(2)}) collective-permute-start(f32[254,8,1]{0,1,2:T(8,128)S(1)} %copy.368), channel_id=1, source_target_pairs={{1,0},{2,1},{3,2},{4,3},{5,4},{6,5},{7,6},{8,7},{9,8},{10,9},{11,1... | collective-permute-start | bytes 24392 | tf_op jit(solution)/shard_map/ppermute | solution.py:33
  235.7 1.4 fusion.28
  237.3 1.3 copy.372
  (294 shorter events, 98.3 us)
Async XLA Ops:
  0.6 103.4 %copy-start = (f32[254,8]{0,1:T(8,128)S(1)}, f32[254,8]{0,1:T(8,128)}, u32[]{:S(2)}) copy-start(f32[254,8]{0,1:T(8,128)} %param.12) | copy-start | bytes 24388
  92.5 11.5 %copy-start.4 = (s32[64]{0:T(128)S(1)}, s32[64]{0:T(128)}, u32[]{:S(2)}) copy-start(s32[64]{0:T(128)} %param.14) | copy-start | bytes 772
  92.5 12.6 %copy-start.3 = (f32[254]{0:T(256)S(1)}, f32[254]{0:T(256)}, u32[]{:S(2)}) copy-start(f32[254]{0:T(256)} %param.13) | copy-start | bytes 3052
  92.5 41.2 %all-to-all-start = ((f32[128,4,1,8,96]{4,3,1,2,0:T(8,128)}), f32[128,4,1,8,96]{4,3,1,2,0:T(8,128)S(1)}, u32[]{:S(2)}, u32[]{:S(2)}) async-start(f32[128,4,1,8,96]{4,3,1,2,0:T(8,128)} %constant_dynamic-update-slice_fusion), calls=%async_computation | async-start | bytes 4194304 | tf_op jit(solution)/shard_map/all_to_all | solution.py:16
  133.7 1.4 copy-start.1
  182.8 4.8 %copy-start.2 = (s32[254,1]{0,1:T(1,128)S(1)}, s32[254,1]{0,1:T(1,128)}, u32[]{:S(2)}) copy-start(s32[254,1]{0,1:T(1,128)} %param.15) | copy-start | bytes 3052
  182.8 34.6 %all-to-all-start.1 = ((f32[4,128,8,96]{3,2,0,1:T(8,128)}), f32[4,128,8,96]{3,2,0,1:T(8,128)S(1)}, u32[]{:S(2)}, u32[]{:S(2)}) async-start(f32[4,128,8,96]{3,2,0,1:T(8,128)} %copy.366), calls=%async_computation.1 | async-start | bytes 4194304 | tf_op jit(solution)/shard_map/all_to_all | solution.py:137
  222.7 12.9 %collective-permute-start = (f32[254,1,96]{2,1,0:T(1,128)}, f32[254,1,96]{2,1,0:T(1,128)S(1)}, u32[]{:S(2)}, u32[]{:S(2)}) collective-permute-start(f32[254,1,96]{2,1,0:T(1,128)} %get-tuple-element.218), channel_id=1, source_target_pairs={{16,0},{32,16},{48,32},{64,48},{80,64},{96,80},{112,96},{17,1},{33... | collective-permute-start | bytes 292616 | tf_op jit(solution)/shard_map/ppermute | solution.py:33
  225.8 9.9 %collective-permute-start.1 = (f32[254,1,96]{2,1,0:T(1,128)S(1)}, f32[254,1,96]{2,1,0:T(1,128)S(1)}, u32[]{:S(2)}, u32[]{:S(2)}) collective-permute-start(f32[254,1,96]{2,1,0:T(1,128)S(1)} %get-tuple-element.219), channel_id=1, source_target_pairs={{0,16},{16,32},{32,48},{48,64},{64,80},{80,96},{96,112},{1,17},{17... | collective-permute-start | bytes 292616 | tf_op jit(solution)/shard_map/ppermute | solution.py:30
  229.1 6.1 %collective-permute-start.3 = (f32[254,8,1]{0,1,2:T(8,128)S(1)}, f32[254,8,1]{0,1,2:T(8,128)S(1)}, u32[]{:S(2)}, u32[]{:S(2)}) collective-permute-start(f32[254,8,1]{0,1,2:T(8,128)S(1)} %copy.370), channel_id=1, source_target_pairs={{0,1},{1,2},{2,3},{3,4},{4,5},{5,6},{6,7},{7,8},{8,9},{9,10},{10,1... | collective-permute-start | bytes 24392 | tf_op jit(solution)/shard_map/ppermute | solution.py:30
  229.6 5.1 %collective-permute-start.2 = (f32[254,8,1]{0,1,2:T(8,128)S(1)}, f32[254,8,1]{0,1,2:T(8,128)S(1)}, u32[]{:S(2)}, u32[]{:S(2)}) collective-permute-start(f32[254,8,1]{0,1,2:T(8,128)S(1)} %copy.368), channel_id=1, source_target_pairs={{1,0},{2,1},{3,2},{4,3},{5,4},{6,5},{7,6},{8,7},{9,8},{10,9},{11,1... | collective-permute-start | bytes 24392 | tf_op jit(solution)/shard_map/ppermute | solution.py:33
